TPU v7x, 32 devices: a whole 2x2x4 slice. The times are simulated.
32 devices in a mesh: ens: 2 (over x), lat: 4 (over y, core), lon: 4 (over z).
Axes of the slice: x: 2, y: 2, z: 4, core: 2. Of those that a mesh axis runs over, the one named last changes fastest.
Arguments:
- starting_state: bfloat16 [4, 222, 128, 512], P('ens', None, 'lat', 'lon'), may hold values from -6 to 6
- random_fields: bfloat16 [4, 16, 128, 512], P('ens', None, 'lat', 'lon'), may hold values from -6 to 6
- observed: float32 [6, 13, 128, 512], P(None, None, 'lat', 'lon'), may hold values from -6 to 6
- input_weight: bfloat16 [256, 222], replicated, may hold values from -0.375 to 0.375
- random_weight: bfloat16 [256, 16], replicated, may hold values from -1.5 to 1.5
- hidden_weight: bfloat16 [256, 256], replicated, may hold values from -0.375 to 0.375
- output_weight: bfloat16 [222, 256], replicated, may hold values from -0.375 to 0.375
- diffusivity: float32 [222], replicated, may hold values from 0.02 to 0.24
Outputs:
- grad_state: bfloat16 [4, 222, 128, 512], P('ens', None, 'lat', 'lon')
- grad_w_in: float32 [256, 222], replicated
- grad_w_noise: float32 [256, 16], replicated
- grad_w_mid: float32 [256, 256], replicated
- grad_w_out: float32 [222, 256], replicated
- grad_diffusivity: float32 [222], replicated
All inputs are finite; a program needn't handle non-finite values.
Results may differ from a plain program's by a relative error of at most 0.008.
Values may be sent and summed in bfloat16 or wider, within the bound.
No kernel may reach another device: no remote copies, remote signals or barrier semaphores. Data moves between devices by JAX's collectives and lax.ppermute only.
A program may use at most 128 MiB of HBM per device.

v0:
```python
import jax
import jax.numpy as jnp
from jax import lax
from jax.sharding import PartitionSpec as P

PROGNOSTIC_COUNT = 6
LEVEL_COUNT = 37
SCORED = 13
DELTA = 0.1


def with_halo(block, sides, width):
    for axis, dim in sides:
        count = lax.axis_size(axis)
        forward = [(i, i + 1) for i in range(count - 1)]
        forward.append((count - 1, 0))
        backward = [(target, source) for source, target in forward]
        low = lax.ppermute(
            lax.slice_in_dim(block, block.shape[dim] - width, None, axis=dim), axis, forward
        )
        high = lax.ppermute(lax.slice_in_dim(block, 0, width, axis=dim), axis, backward)
        block = jnp.concatenate([low, block, high], axis=dim)
    return block


def softened_slope(diff):
    return diff * lax.rsqrt(diff * diff + DELTA * DELTA)


def silu_slope(value):
    gate = jax.nn.sigmoid(value)
    return gate * (1.0 + value * (1.0 - gate))


def pole_mask(padded):
    lat_id = lax.axis_index("lat")
    lat_count = lax.axis_size("lat")
    row_ids = jnp.arange(padded.shape[2])
    dropped = (row_ids == 0) & (lat_id == 0) | (row_ids == padded.shape[2] - 1) & (
        lat_id == lat_count - 1
    )
    return padded * jnp.logical_not(dropped)[:, None].astype(padded.dtype)


def stencil(padded, field):
    return (
        padded[:, :, 2:, 1:-1]
        + padded[:, :, :-2, 1:-1]
        + padded[:, :, 1:-1, 2:]
        + padded[:, :, 1:-1, :-2]
        - 4.0 * field
    )


def on_device(
    starting_state,
    random_fields,
    observed,
    input_weight,
    random_weight,
    hidden_weight,
    output_weight,
    diffusivity,
):
    resident_members, channels, latitude_rows, longitude_columns = starting_state.shape
    cells = latitude_rows * longitude_columns
    hidden_width = hidden_weight.shape[0]
    evaluated_rows = PROGNOSTIC_COUNT * SCORED
    padded_state = pole_mask(with_halo(starting_state, (("lat", 2), ("lon", 3)), 1))
    start = starting_state.astype(jnp.float32)
    laplacian_initial = stencil(padded_state.astype(jnp.float32), start)
    stepped = start + diffusivity[None, :, None, None] * laplacian_initial
    advanced_partner = stepped.astype(jnp.bfloat16).reshape(resident_members, channels, cells)
    random_flattened = random_fields.reshape(resident_members, random_fields.shape[1], cells)
    first_preactivation = jnp.einsum(
        "hc,mcn->mhn", input_weight, advanced_partner, preferred_element_type=jnp.float32
    )
    first_preactivation = first_preactivation + jnp.einsum(
        "hk,mkn->mhn", random_weight, random_flattened, preferred_element_type=jnp.float32
    )
    first_activation = jax.nn.silu(first_preactivation).astype(jnp.bfloat16)
    second_preactivation = jnp.einsum(
        "hk,mkn->mhn", hidden_weight, first_activation, preferred_element_type=jnp.float32
    )
    second_activation = jax.nn.silu(second_preactivation).astype(jnp.bfloat16)
    w_out_scored = output_weight.reshape(PROGNOSTIC_COUNT, LEVEL_COUNT, hidden_width)[
        :, ::3
    ].reshape(evaluated_rows, hidden_width)
    advanced_evaluated = stepped.reshape(resident_members, PROGNOSTIC_COUNT, LEVEL_COUNT, cells)[
        :, :, ::3
    ].reshape(resident_members, evaluated_rows, cells)
    member_prediction = advanced_evaluated + jnp.einsum(
        "ch,mhn->mcn", w_out_scored, second_activation, preferred_element_type=jnp.float32
    )
    member_prediction = member_prediction.astype(jnp.bfloat16).reshape(
        resident_members, evaluated_rows, latitude_rows, longitude_columns
    )
    observed_target = observed.reshape(evaluated_rows, latitude_rows, longitude_columns)
    own_values = member_prediction.astype(jnp.float32)
    shard_values = lax.all_gather(member_prediction, "ens", axis=0, tiled=True).astype(jnp.float32)

    def accumulate_member(member_index, running):
        partner_member = lax.dynamic_index_in_dim(shard_values, member_index, 0, keepdims=False)
        return running + softened_slope(own_values - partner_member)

    pairwise_sum = lax.fori_loop(
        0, shard_values.shape[0], accumulate_member, jnp.zeros_like(own_values)
    )
    member_count = resident_members * lax.axis_size("ens")
    score_gradient = (
        softened_slope(own_values - observed_target[None]) - pairwise_sum / (member_count - 1.0)
    ).astype(jnp.bfloat16)
    grad_flat = score_gradient.reshape(resident_members, evaluated_rows, cells)
    out_term = jnp.einsum(
        "mcn,mhn->ch", grad_flat, second_activation, preferred_element_type=jnp.float32
    )
    back_second = jnp.einsum(
        "ch,mcn->mhn", w_out_scored, grad_flat, preferred_element_type=jnp.float32
    )
    delta_second = (back_second * silu_slope(second_preactivation)).astype(jnp.bfloat16)
    mid_term = jnp.einsum(
        "mhn,mkn->hk", delta_second, first_activation, preferred_element_type=jnp.float32
    )
    back_first = jnp.einsum(
        "hk,mhn->mkn", hidden_weight, delta_second, preferred_element_type=jnp.float32
    )
    delta_first = (back_first * silu_slope(first_preactivation)).astype(jnp.bfloat16)
    in_term = jnp.einsum(
        "mhn,mcn->hc", delta_first, advanced_partner, preferred_element_type=jnp.float32
    )
    noise_term = jnp.einsum(
        "mhn,mkn->hk", delta_first, random_flattened, preferred_element_type=jnp.float32
    )
    grad_stepped = jnp.einsum(
        "hc,mhn->mcn", input_weight, delta_first, preferred_element_type=jnp.float32
    )
    grad_stepped = (
        grad_stepped.reshape(resident_members, PROGNOSTIC_COUNT, LEVEL_COUNT, cells)
        .at[:, :, ::3]
        .add(
            grad_flat.astype(jnp.float32).reshape(resident_members, PROGNOSTIC_COUNT, SCORED, cells)
        )
    )
    grad_stepped = grad_stepped.reshape(
        resident_members, channels, latitude_rows, longitude_columns
    )
    diffusivity_term = jnp.sum(grad_stepped * laplacian_initial, axis=(0, 2, 3))
    in_term, noise_term, mid_term, out_term, diffusivity_term = lax.psum(
        (in_term, noise_term, mid_term, out_term, diffusivity_term), ("ens", "lat", "lon")
    )
    padded_grad = pole_mask(
        with_halo(grad_stepped.astype(jnp.bfloat16), (("lat", 2), ("lon", 3)), 1).astype(
            grad_stepped.dtype
        )
    )
    grad_laplace = stencil(padded_grad, grad_stepped)
    grad_state = (grad_stepped + diffusivity[None, :, None, None] * grad_laplace).astype(
        jnp.bfloat16
    )
    inverse_count = 1.0 / (
        resident_members
        * lax.axis_size("ens")
        * latitude_rows
        * lax.axis_size("lat")
        * longitude_columns
        * lax.axis_size("lon")
    )
    grad_w_out = (
        jnp.zeros((PROGNOSTIC_COUNT, LEVEL_COUNT, hidden_width), jnp.float32)
        .at[:, ::3]
        .set(out_term.reshape(PROGNOSTIC_COUNT, SCORED, hidden_width))
        .reshape(channels, hidden_width)
    )
    return (
        grad_state,
        in_term * inverse_count,
        noise_term * inverse_count,
        mid_term * inverse_count,
        grad_w_out * inverse_count,
        diffusivity_term * inverse_count,
    )


def solution(mesh):
    in_specs = (
        P("ens", None, "lat", "lon"),
        P("ens", None, "lat", "lon"),
        P(None, None, "lat", "lon"),
        P(),
        P(),
        P(),
        P(),
        P(),
    )
    out_specs = (P("ens", None, "lat", "lon"), P(), P(), P(), P(), P())
    return jax.shard_map(
        on_device, mesh=mesh, in_specs=in_specs, out_specs=out_specs, check_vma=False
    )
```

profile of v0, /device:TPU:0, one launch (start us, length us, event | category | flops | bytes accessed | tf_op | source)
XLA Modules:
  0.0 457.5 jit_solution(17218860512130126049)
XLA Ops:
  7.2 1.9 fusion.34
  9.7 2.0 collective-permute-start.1
  12.8 5.2 %fusion.27 = f32[2,4096,256]{2,1,0:T(8,128)} fusion(bf16[2,16,4096]{2,1,0:T(8,128)(2,1)S(1)} %reshape.82, bf16[256,16]{0,1:T(8,128)(2,1)} %param.14), kind=kOutput, calls=%fused_computation.67 | convolution fusion | flops 67108864 | bytes 8658944 | tf_op jit(solution)/shard_map/hk,mkn->mhn/dot_general | solution.py:78
  18.0 8.3 %copy.76 = bf16[2,222,32,128]{1,2,3,0:T(8,128)(2,1)} copy(bf16[2,222,32,128]{3,2,1,0:T(8,128)(2,1)} %param.10) | data formatting | bytes 7274496 | tf_op args[0]
  27.5 2.4 collective-permute-start.2
  29.9 2.4 collective-permute-start.3
  34.5 4.8 %fusion.19 = f32[2,222,34,130]{1,2,3,0:T(8,128)S(1)} fusion(bf16[2,222,34,1]{1,2,3,0:T(8,128)(2,1)S(1)} %collective-permute-done.3, bf16[2,222,1,128]{1,2,3,0:T(2,128)(2,1)S(1)} %copy.81, bf16[2,222,32,128]{1,2,3,0:T(8,128)(2,1)} %copy.76, bf16[2,222,1,128]{1,2,3,0:T(2,128)(2,1)S(1)} %copy.79, bf16[2,222,34,1]{1,2,3,0:T(8,128)(2,1)S(1)} %collective-permute-done.2, ...), kind=kLoop, calls=%fused_computation.44 | loop fusion | flops 23549760 | bytes 11774948 | tf_op jit(solution)/shard_map/convert_element_type | solution.py:71
  39.3 11.2 %fusion.31 = (bf16[2,222,32,128]{1,2,3,0:T(8,128)(2,1)}, f32[2,222,32,128]{1,2,3,0:T(8,128)}, f32[2,222,32,128]{1,2,3,0:T(8,128)}) fusion(f32[222]{0:T(256)S(1)} %copy-done.10, bf16[2,222,32,128]{1,2,3,0:T(8,128)(2,1)} %copy.76, f32[2,222,34,130]{1,2,3,0:T(8,128)S(1)} %fusion.19), kind=kLoop, calls=%fused_computation.75 | loop fusion | flops 16367616 | bytes 50922360 | tf_op jit(solution)/shard_map/convert_element_type | solution.py:73
  50.5 8.3 %copy.83 = bf16[2,222,32,128]{3,2,1,0:T(8,128)(2,1)} copy(bf16[2,222,32,128]{1,2,3,0:T(8,128)(2,1)} %get-tuple-element.126) | data formatting | bytes 7274496 | tf_op jit(solution)/shard_map/convert_element_type | solution.py:73
  58.8 4.4 reshape.81
  63.2 10.1 %copy.82 = f32[2,222,32,128]{3,2,0,1:T(8,128)} copy(f32[2,222,32,128]{1,2,3,0:T(8,128)} %get-tuple-element.127) | data formatting | bytes 14548992 | tf_op jit(solution)/shard_map/add | solution.py:72
  73.3 10.0 %reshape.79 = f32[2,6,37,4096]{3,0,2,1:T(2,128)} reshape(f32[2,222,32,128]{3,2,0,1:T(8,128)} %copy.82) | data formatting | bytes 14548992 | tf_op jit(solution)/shard_map/reshape | solution.py:89
  83.3 2.0 slice.62
  85.4 9.0 %fusion.16 = (bf16[2,256,4096]{1,2,0:T(8,128)(2,1)S(1)}, f32[2,4096,256]{2,1,0:T(8,128)}) fusion(f32[2,4096,256]{2,1,0:T(8,128)} %fusion.27, bf16[2,222,4096]{2,1,0:T(8,128)(2,1)} %reshape.81, bf16[256,222]{0,1:T(8,128)(2,1)S(1)} %copy-done.8), kind=kOutput, calls=%fused_computation.37 | convolution fusion | flops 943718400 | bytes 24722432 | tf_op jit(solution)/shard_map/hc,mcn->mhn/dot_general | solution.py:75
  94.4 4.7 %fusion.10 = (bf16[2,256,4096]{1,2,0:T(8,128)(2,1)S(1)}, f32[2,4096,256]{2,1,0:T(8,128)}) fusion(bf16[2,256,4096]{1,2,0:T(8,128)(2,1)S(1)} %get-tuple-element.139, bf16[256,256]{1,0:T(8,128)(2,1)S(1)} %copy-done), kind=kOutput, calls=%fused_computation.28 | convolution fusion | flops 1084227584 | bytes 16908288 | tf_op jit(solution)/shard_map/hk,mkn->mhn/dot_general | solution.py:82
  99.1 2.0 copy-done.3
  101.1 2.0 fusion.21
  105.3 3.2 convert_element_type.74
  108.5 36.1 %all-gather.2.cloned.1.call-done = bf16[4,78,32,128]{3,2,1,0:T(8,128)(2,1)} async-done(((bf16[2,78,32,128]{3,2,1,0:T(8,128)(2,1)}), bf16[4,78,32,128]{3,2,1,0:T(8,128)(2,1)}) %all-gather.2.cloned.1.call-update) | async-done | bytes 2555920 | tf_op jit(solution)/shard_map/all_gather | solution.py:100
  144.6 4.8 %convert_element_type.75 = f32[4,78,32,128]{3,2,1,0:T(8,128)} convert(bf16[4,78,32,128]{3,2,1,0:T(8,128)(2,1)} %all-gather.2.cloned.1.call-done) | non-fusion elementwise | flops 1277952 | bytes 7667712 | tf_op jit(solution)/shard_map/convert_element_type | solution.py:100
  149.4 24.0 %while.14 = (s32[]{:T(128)}, f32[2,78,32,128]{3,2,1,0:T(8,128)}, f32[4,78,32,128]{3,2,1,0:T(8,128)}, f32[2,78,32,128]{3,2,1,0:T(8,128)}, s32[]{:T(128)}, /*index=5*/s32[]{:T(128)}) while((s32[]{:T(128)}, f32[2,78,32,128]{3,2,1,0:T(8,128)}, f32[4,78,32,128]{3,2,1,0:T(8,128)}, f32[2,78,32,128]{3,2,1,0:T(8,128)}, s32[]{:T(128)}, ...), condition=%wide.region_1.2_spmd.clone, body=%wide.region_0.1_spmd.clone.sunk | while | flops 3833859 | bytes 11501651 | solution.py:106
  150.9 4.0 select_add_fusion.2
  156.3 4.8 %select_add_fusion.2 = f32[2,78,32,128]{3,2,1,0:T(8,128)} fusion(f32[2,78,32,128]{3,2,1,0:T(8,128)} %get-tuple-element.175, f32[2,78,32,128]{3,2,1,0:T(8,128)} %get-tuple-element.183, f32[78,32,128]{2,1,0:T(8,128)S(1)} %dynamic-slice_bitcast_fusion.2, pred[]{:T(512)S(6)} %compare.3), kind=kLoop, calls=%fused_computation.2.clone.1 | loop fusion | flops 3833856 | bytes 8945665 | tf_op jit(solution)/shard_map/while/body/eval_jaxpr/add | solution.py:104
  162.5 4.8 %select_add_fusion.2 = f32[2,78,32,128]{3,2,1,0:T(8,128)} fusion(f32[2,78,32,128]{3,2,1,0:T(8,128)} %get-tuple-element.175, f32[2,78,32,128]{3,2,1,0:T(8,128)} %get-tuple-element.183, f32[78,32,128]{2,1,0:T(8,128)S(1)} %dynamic-slice_bitcast_fusion.2, pred[]{:T(512)S(6)} %compare.3), kind=kLoop, calls=%fused_computation.2.clone.1 | loop fusion | flops 3833856 | bytes 8945665 | tf_op jit(solution)/shard_map/while/body/eval_jaxpr/add | solution.py:104
  168.7 4.8 %select_add_fusion.2 = f32[2,78,32,128]{3,2,1,0:T(8,128)} fusion(f32[2,78,32,128]{3,2,1,0:T(8,128)} %get-tuple-element.175, f32[2,78,32,128]{3,2,1,0:T(8,128)} %get-tuple-element.183, f32[78,32,128]{2,1,0:T(8,128)S(1)} %dynamic-slice_bitcast_fusion.2, pred[]{:T(512)S(6)} %compare.3), kind=kLoop, calls=%fused_computation.2.clone.1 | loop fusion | flops 3833856 | bytes 8945665 | tf_op jit(solution)/shard_map/while/body/eval_jaxpr/add | solution.py:104
  173.4 2.8 subtract_convert_fusion
  177.0 3.2 convolution_bitcast_fusion.4
  180.2 6.4 %fusion.6 = bf16[2,256,4096]{1,2,0:T(8,128)(2,1)S(1)} fusion(f32[2,4096,256]{2,1,0:T(8,128)} %get-tuple-element.142, bf16[2,78,4096]{2,1,0:T(8,128)(2,1)S(1)} %reshape.86, bf16[78,256,1]{1,0,2:T(8,128)(2,1)S(1)} %reshape.110), kind=kOutput, calls=%fused_computation.21 | convolution fusion | flops 346030080 | bytes 13900800 | tf_op jit(solution)/shard_map/ch,mcn->mhn/dot_general | solution.py:117
  186.6 2.0 convolution_bitcast_fusion.2
  188.6 3.5 fusion.5
  192.2 1.8 convolution_bitcast_fusion.3
  194.0 4.4 convolution_bitcast_fusion
  198.4 1.8 copy.88
  200.9 11.8 %copy.87 = f32[2,222,4096]{2,0,1:T(2,128)} copy(f32[2,222,4096]{2,1,0:T(8,128)} %convolution_bitcast_fusion) | data formatting | bytes 14548992 | tf_op jit(solution)/shard_map/hc,mhn->mcn/transpose | solution.py:134
  212.7 2.4 reshape.92
  215.1 1.9 copy.89
  217.0 16.4 %scatter_fusion = f32[2,6,37,4096]{3,0,2,1:T(2,128)} fusion(f32[2,6,37,4096]{3,0,2,1:T(2,128)} %bitcast.129, s32[13]{0:T(128)S(1)} %multiply_bitcast_fusion, f32[13,2,6,4096]{3,1,2,0:T(2,128)S(1)} %copy.89), kind=kCustom, calls=%fused_computation | custom fusion | flops 638976 | bytes 7667764 | tf_op jit(solution)/shard_map/scatter-add | solution.py:140
  233.4 10.9 %reshape.88 = f32[2,222,32,128]{3,2,0,1:T(8,128)} reshape(f32[2,6,37,4096]{3,0,2,1:T(2,128)} %scatter_fusion) | data formatting | bytes 14548992 | tf_op jit(solution)/shard_map/reshape | solution.py:144
  244.3 10.1 %copy.96 = f32[2,222,32,128]{1,2,3,0:T(8,128)} copy(f32[2,222,32,128]{3,2,0,1:T(8,128)} %reshape.88) | data formatting | bytes 14548992 | tf_op jit(solution)/shard_map/reshape | solution.py:144
  254.4 10.2 %multiply_reduce_fusion = (f32[222]{0:T(256)S(1)}, bf16[2,222,32,128]{1,2,3,0:T(8,128)(2,1)S(1)}) fusion(f32[2,222,32,128]{1,2,3,0:T(8,128)} %copy.96, f32[2,222,32,128]{1,2,3,0:T(8,128)} %get-tuple-element.128), kind=kLoop, calls=%fused_computation.40 | loop fusion | flops 5455650 | bytes 18187128 | tf_op jit(solution)/shard_map/reduce_sum | solution.py:147
  264.6 2.0 copy-done.1
  267.4 1.8 collective-permute-start.5
  269.2 39.4 %all-reduce = (f32[256,16]{0,1:T(8,128)S(1)}, f32[222]{0:T(256)S(1)}) all-reduce(f32[256,16]{0,1:T(8,128)S(1)} %convolution_bitcast_fusion.5, f32[222]{0:T(256)S(1)} %get-tuple-element.129), channel_id=1, replica_groups=mesh['ens'=2,'lat'=4,'lon'=4] {'ens','lat','lon'}, use_global_device_ids=true, to_apply=%region_4.5 | all-reduce | flops 4318 | bytes 34544 | tf_op jit(solution)/shard_map/psum | solution.py:148
  312.0 2.4 collective-permute-start.7
  316.4 8.6 %convert_multiply_fusion = f32[2,222,34,130]{1,2,3,0:T(8,128)} fusion(bf16[2,222,34,1]{1,2,3,0:T(8,128)(2,1)S(1)} %collective-permute-done.7, bf16[2,222,1,128]{1,2,3,0:T(2,128)(2,1)S(1)} %copy.94, bf16[2,222,32,128]{1,2,3,0:T(8,128)(2,1)} %copy-done.1, bf16[2,222,1,128]{1,2,3,0:T(2,128)(2,1)S(1)} %copy.93, ...), kind=kLoop, calls=%fused_computation.4 | loop fusion | flops 21587280 | bytes 11775016 | tf_op jit(solution)/shard_map/mul | solution.py:42
  325.0 19.3 %fusion.4 = bf16[2,222,32,128]{1,2,3,0:T(8,128)(2,1)} fusion(f32[2,222,32,128]{1,2,3,0:T(8,128)} %copy.96, f32[2,222,34,130]{1,2,3,0:T(8,128)} %convert_multiply_fusion, f32[222]{0:T(256)S(1)} %copy-done.10), kind=kLoop, calls=%fused_computation.12 | loop fusion | flops 14548992 | bytes 40010616 | tf_op jit(solution)/shard_map/convert_element_type | solution.py:157
  344.3 8.3 %copy.105 = bf16[2,222,32,128]{3,2,1,0:T(8,128)(2,1)} copy(bf16[2,222,32,128]{1,2,3,0:T(8,128)(2,1)} %fusion.4) | data formatting | bytes 7274496
  352.6 92.1 %all-reduce.4.cloned.1.call-done = (f32[256,222]{0,1:T(8,128)}, f32[256,256]{1,0:T(8,128)}, f32[6,13,256]{2,0,1:T(8,128)}) async-done(((f32[256,222]{0,1:T(8,128)}, f32[256,256]{1,0:T(8,128)}, f32[6,13,256]{2,0,1:T(8,128)}), (f32[256,222]{0,1:T(8,128)}, f32[256,256]{1,0:T(8,128)}, f32[6,13,256]{2,0,1:T(8,128)})) %all-reduce.4.cloned.1.call-update) | async-done | bytes 569360 | tf_op jit(solution)/shard_map/psum | solution.py:148
  (76 shorter events, 26.3 us)
Async XLA Ops:
  7.2 87.2 %copy-start = (bf16[256,256]{1,0:T(8,128)(2,1)S(1)}, bf16[256,256]{1,0:T(8,128)(2,1)}, u32[]{:S(2)}) copy-start(bf16[256,256]{1,0:T(8,128)(2,1)} %param.15) | copy-start | bytes 393220
  7.2 137.4 %all-gather.2.cloned.1.call-start = ((), (), s32[]{:S(2)}) async-start(), calls=%async_computation | async-start | bytes 3833856 | tf_op jit(solution)/shard_map/all_gather | solution.py:100
  9.1 17.2 %collective-permute-start = (bf16[2,222,1,128]{3,1,2,0:T(8,128)(2,1)S(1)}, bf16[2,222,1,128]{3,1,2,0:T(8,128)(2,1)S(1)}, u32[]{:S(2)}, u32[]{:S(2)}) collective-permute-start(bf16[2,222,1,128]{3,1,2,0:T(8,128)(2,1)S(1)} %copy.113), channel_id=1, source_target_pairs={{0,4},{4,8},{8,12},{12,0},{1,5},{5,9},{9,13},{13,1},{2,6},{6,10},{... | collective-permute-start | bytes 341000 | tf_op jit(solution)/shard_map/ppermute | solution.py:18
  9.7 16.8 %collective-permute-start.1 = (bf16[2,222,1,128]{3,1,2,0:T(8,128)(2,1)S(1)}, bf16[2,222,1,128]{3,1,2,0:T(8,128)(2,1)S(1)}, u32[]{:S(2)}, u32[]{:S(2)}) collective-permute-start(bf16[2,222,1,128]{3,1,2,0:T(8,128)(2,1)S(1)} %copy.114), channel_id=1, source_target_pairs={{4,0},{8,4},{12,8},{0,12},{5,1},{9,5},{13,9},{1,13},{6,2},{10,6},{... | collective-permute-start | bytes 341000 | tf_op jit(solution)/shard_map/ppermute | solution.py:21
  18.0 14.3 %copy-start.9 = (bf16[222,256]{1,0:T(8,128)(2,1)S(1)}, bf16[222,256]{1,0:T(8,128)(2,1)}, u32[]{:S(2)}) copy-start(bf16[222,256]{1,0:T(8,128)(2,1)} %param.16) | copy-start | bytes 340996
  27.5 6.5 %collective-permute-start.2 = (bf16[2,222,34,1]{1,2,3,0:T(8,128)(2,1)S(1)}, bf16[2,222,34,1]{1,2,3,0:T(8,128)(2,1)S(1)}, u32[]{:S(2)}, u32[]{:S(2)}) collective-permute-start(bf16[2,222,34,1]{1,2,3,0:T(8,128)(2,1)S(1)} %get-tuple-element.133), channel_id=1, source_target_pairs={{0,1},{1,2},{2,3},{3,0},{4,5},{5,6},{6,7},{7,4},{8,9},{9,10},{10,1... | collective-permute-start | bytes 90584 | tf_op jit(solution)/shard_map/ppermute | solution.py:18
  29.9 4.5 collective-permute-start.3
  32.4 6.8 %copy-start.10 = (f32[222]{0:T(256)S(1)}, f32[222]{0:T(256)}, u32[]{:S(2)}) copy-start(f32[222]{0:T(256)} %param.17) | copy-start | bytes 2668
  73.3 12.0 %copy-start.8 = (bf16[256,222]{0,1:T(8,128)(2,1)S(1)}, bf16[256,222]{0,1:T(8,128)(2,1)}, u32[]{:S(2)}) copy-start(bf16[256,222]{0,1:T(8,128)(2,1)} %param.13) | copy-start | bytes 340996
  94.4 4.7 %copy-start.4 = (bf16[2,256,4096]{1,2,0:T(8,128)(2,1)}, bf16[2,256,4096]{1,2,0:T(8,128)(2,1)S(1)}, u32[]{:S(2)}) copy-start(bf16[2,256,4096]{1,2,0:T(8,128)(2,1)S(1)} %get-tuple-element.139) | copy-start | bytes 12582916
  99.1 2.0 copy-start.3
  104.7 339.9 %all-reduce.4.cloned.1.call-start = ((), (), s32[]{:S(2)}) async-start(), calls=%async_computation.1 | async-start | bytes 1196032 | tf_op jit(solution)/shard_map/psum | solution.py:148
  149.4 24.0 %copy-start.2 = (bf16[2,78,32,128]{3,2,1,0:T(8,128)(2,1)S(1)}, bf16[2,78,32,128]{3,2,1,0:T(8,128)(2,1)}, u32[]{:S(2)}) copy-start(bf16[2,78,32,128]{3,2,1,0:T(8,128)(2,1)} %reshape.85) | copy-start | bytes 3833860
  177.0 11.7 %slice-start = ((s8[8388608]{0:T(1024)(128)(4,1)}), s8[4194304]{0:T(1024)(128)(4,1)S(1)}, s32[]{:S(2)}) async-start(s8[8388608]{0:T(1024)(128)(4,1)} %bitcast.134), calls=%async_computation.2 | async-start | bytes 8388608
  180.2 6.5 %copy-start.5 = (bf16[2,256,4096]{1,2,0:T(8,128)(2,1)S(1)}, bf16[2,256,4096]{1,2,0:T(8,128)(2,1)}, u32[]{:S(2)}) copy-start(bf16[2,256,4096]{1,2,0:T(8,128)(2,1)} %copy-done.4) | copy-start | bytes 12582916
  180.2 8.5 %slice-start.1 = ((s8[8388608]{0:T(1024)(128)(4,1)}), s8[4194304]{0:T(1024)(128)(4,1)S(1)}, s32[]{:S(2)}) async-start(s8[8388608]{0:T(1024)(128)(4,1)} %bitcast.134), calls=%async_computation.3 | async-start | bytes 8388608
  188.6 3.6 copy-start.7
  200.9 11.8 %copy-start.6 = (f32[2,78,32,128]{3,2,0,1:T(8,128)S(1)}, f32[2,78,32,128]{3,2,0,1:T(8,128)}, u32[]{:S(2)}) copy-start(f32[2,78,32,128]{3,2,0,1:T(8,128)} %copy.88) | copy-start | bytes 7667716
  264.6 2.0 copy-start.1
  267.2 42.1 %collective-permute-start.4 = (bf16[2,222,1,128]{3,1,2,0:T(8,128)(2,1)S(1)}, bf16[2,222,1,128]{3,1,2,0:T(8,128)(2,1)S(1)}, u32[]{:S(2)}, u32[]{:S(2)}) collective-permute-start(bf16[2,222,1,128]{3,1,2,0:T(8,128)(2,1)S(1)} %copy.91), channel_id=1, source_target_pairs={{0,4},{4,8},{8,12},{12,0},{1,5},{5,9},{9,13},{13,1},{2,6},{6,10},{... | collective-permute-start | bytes 341000 | tf_op jit(solution)/shard_map/ppermute | solution.py:18
  267.4 42.0 %collective-permute-start.5 = (bf16[2,222,1,128]{3,1,2,0:T(8,128)(2,1)S(1)}, bf16[2,222,1,128]{3,1,2,0:T(8,128)(2,1)S(1)}, u32[]{:S(2)}, u32[]{:S(2)}) collective-permute-start(bf16[2,222,1,128]{3,1,2,0:T(8,128)(2,1)S(1)} %copy.92), channel_id=1, source_target_pairs={{4,0},{8,4},{12,8},{0,12},{5,1},{9,5},{13,9},{1,13},{6,2},{10,6},{... | collective-permute-start | bytes 341000 | tf_op jit(solution)/shard_map/ppermute | solution.py:21
  310.5 6.0 %collective-permute-start.6 = (bf16[2,222,34,1]{1,2,3,0:T(8,128)(2,1)S(1)}, bf16[2,222,34,1]{1,2,3,0:T(8,128)(2,1)S(1)}, u32[]{:S(2)}, u32[]{:S(2)}) collective-permute-start(bf16[2,222,34,1]{1,2,3,0:T(8,128)(2,1)S(1)} %get-tuple-element.131), channel_id=1, source_target_pairs={{0,1},{1,2},{2,3},{3,0},{4,5},{5,6},{6,7},{7,4},{8,9},{9,10},{10,1... | collective-permute-start | bytes 90584 | tf_op jit(solution)/shard_map/ppermute | solution.py:18
  312.0 4.4 collective-permute-start.7
Sparse Core Ops, SparseCore 0:
  104.9 39.6 all-gather.1
  315.8 128.8 all-reduce.3
where the time goes:
time: 463 us; the launch traced here: 458 us
  waiting for transfers between devices  131 us (28%)
  local copies, waits for them, and re-layouts  110 us (24%)
  other arithmetic  106 us (23%)
  matrix products  43 us (9%)
  blocking collectives  39.4 us (9%)
  between operations  14.6 us (3%)
  starting transfers between devices  13.7 us (3%)
    psum x1, waiting for transfers between devices, on_device(): lax.psum((in_term, noise_term, mid_term, out_term, diffusivity_term), ('e...  92.1 us
    psum x1, blocking collectives, on_device(): lax.psum((in_term, noise_term, mid_term, out_term, diffusivity_term), ('e...  39.4 us
    all_gather x1, waiting for transfers between devices, on_device(): lax.all_gather(member_prediction, 'ens', axis=0, tiled=True)  36.1 us
    reshape x2, local copies, waits for them, and re-layouts, on_device(): grad_stepped.reshape(resident_members, channels, latitude_rows, longitude...  20.9 us
    unnamed x30, local copies, waits for them, and re-layouts  20.7 us
    convert_element_type x1, other arithmetic, on_device(): (grad_stepped + diffusivity[None, :, None, None] * grad_laplace).astype(j...  19.3 us
    add x4, other arithmetic, accumulate_member(): return running + softened_slope(own_values - partner_member)  18.3 us
    scatter-add x1, other arithmetic, on_device(): grad_stepped = grad_stepped.reshape(resident_members, PROGNOSTIC_COUNT, L...  16.4 us
  transfers between devices with their start and end apart: 10, of which 5 were waited for; matrix products, arithmetic and copies ran while one was open for 12% of the time, Pallas kernels for 0%

commit v1 on v0

--- a/solution.py
+++ b/solution.py
@@ -146,7 +146,7 @@
     )
     diffusivity_term = jnp.sum(grad_stepped * laplacian_initial, axis=(0, 2, 3))
     in_term, noise_term, mid_term, out_term, diffusivity_term = lax.psum(
-        (in_term, noise_term, mid_term, out_term, diffusivity_term), ("ens", "lat", "lon")
+        lax.psum((in_term, noise_term, mid_term, out_term, diffusivity_term), ("lat", "lon")), "ens"
     )
     padded_grad = pole_mask(
         with_halo(grad_stepped.astype(jnp.bfloat16), (("lat", 2), ("lon", 3)), 1).astype(

time: 463 us -> 489 us (1.056)
  blocking collectives: 39.4 us -> 68 us
  waiting for transfers between devices: 131 us -> 123 us
    psum x1 -> x2, blocking collectives: 39.4 us -> 68 us  [the longest x1 60.7 us: on_device(): lax.psum((in_term, noise_term, mid_term, out_term, diffusivity_term), ('l...]
    psum x1 -> x2, waiting for transfers between devices: 92.1 us -> 84 us  [the longest x1 80.8 us: on_device(): lax.psum((in_term, noise_term, mid_term, out_term, diffusivity_term), ('l...]
    unnamed x30 -> x34, local copies, waits for them, and re-layouts: 20.7 us -> 22.7 us
  transfers between devices with their start and end apart: 10 -> 11, of which waited for: 5 -> 6; matrix products, arithmetic and copies ran while one was open for 12% -> 12% of each run, Pallas kernels for 0% -> 0%
where the time goes in v1:
time: 489 us; the launch traced here: 484 us
  waiting for transfers between devices  123 us (25%)
  local copies, waits for them, and re-layouts  113 us (23%)
  other arithmetic  106 us (22%)
  blocking collectives  68 us (14%)
  matrix products  45.9 us (9%)
  between operations  14.3 us (3%)
  starting transfers between devices  13.7 us (3%)
    psum x1, waiting for transfers between devices, on_device(): lax.psum((in_term, noise_term, mid_term, out_term, diffusivity_term), ('l...  80.8 us
    psum x1, blocking collectives, on_device(): lax.psum((in_term, noise_term, mid_term, out_term, diffusivity_term), ('l...  60.7 us
    all_gather x1, waiting for transfers between devices, on_device(): lax.all_gather(member_prediction, 'ens', axis=0, tiled=True)  36 us
    unnamed x34, local copies, waits for them, and re-layouts  22.7 us
    reshape x2, local copies, waits for them, and re-layouts, on_device(): grad_stepped.reshape(resident_members, channels, latitude_rows, longitude...  20.9 us
    convert_element_type x1, other arithmetic, on_device(): (grad_stepped + diffusivity[None, :, None, None] * grad_laplace).astype(j...  19.4 us
    add x4, other arithmetic, accumulate_member(): return running + softened_slope(own_values - partner_member)  18.3 us
    scatter-add x1, other arithmetic, on_device(): grad_stepped = grad_stepped.reshape(resident_members, PROGNOSTIC_COUNT, L...  16.4 us
  transfers between devices with their start and end apart: 11, of which 6 were waited for; matrix products, arithmetic and copies ran while one was open for 12% of the time, Pallas kernels for 0%

profile of v1, /device:TPU:0, one launch (start us, length us, event | category | flops | bytes accessed | tf_op | source)
XLA Modules:
  0.0 484.3 jit_solution(15133351573015286691)
XLA Ops:
  7.2 1.9 fusion.34
  9.7 2.0 collective-permute-start.1
  12.8 5.2 %fusion.27 = f32[2,4096,256]{2,1,0:T(8,128)} fusion(bf16[2,16,4096]{2,1,0:T(8,128)(2,1)S(1)} %reshape.82, bf16[256,16]{0,1:T(8,128)(2,1)} %param.14), kind=kOutput, calls=%fused_computation.67 | convolution fusion | flops 67108864 | bytes 8658944 | tf_op jit(solution)/shard_map/hk,mkn->mhn/dot_general | solution.py:78
  18.0 8.3 %copy.76 = bf16[2,222,32,128]{1,2,3,0:T(8,128)(2,1)} copy(bf16[2,222,32,128]{3,2,1,0:T(8,128)(2,1)} %param.10) | data formatting | bytes 7274496 | tf_op args[0]
  27.5 2.4 collective-permute-start.2
  29.9 2.4 collective-permute-start.3
  34.5 4.8 fusion.19
  39.3 11.3 %fusion.31 = (bf16[2,222,32,128]{1,2,3,0:T(8,128)(2,1)}, f32[2,222,32,128]{1,2,3,0:T(8,128)}, f32[2,222,32,128]{1,2,3,0:T(8,128)}) fusion(f32[222]{0:T(256)S(1)} %copy-done.12, bf16[2,222,32,128]{1,2,3,0:T(8,128)(2,1)} %copy.76, f32[2,222,34,130]{1,2,3,0:T(8,128)S(1)} %fusion.19), kind=kLoop, calls=%fused_computation.75 | loop fusion | flops 16367616 | bytes 50922360 | tf_op jit(solution)/shard_map/convert_element_type | solution.py:73
  50.6 8.3 %copy.83 = bf16[2,222,32,128]{3,2,1,0:T(8,128)(2,1)} copy(bf16[2,222,32,128]{1,2,3,0:T(8,128)(2,1)} %get-tuple-element.131) | data formatting | bytes 7274496 | tf_op jit(solution)/shard_map/convert_element_type | solution.py:73
  58.8 4.4 reshape.81
  63.3 10.1 %copy.82 = f32[2,222,32,128]{3,2,0,1:T(8,128)} copy(f32[2,222,32,128]{1,2,3,0:T(8,128)} %get-tuple-element.132) | data formatting | bytes 14548992 | tf_op jit(solution)/shard_map/add | solution.py:72
  73.4 10.0 %reshape.79 = f32[2,6,37,4096]{3,0,2,1:T(2,128)} reshape(f32[2,222,32,128]{3,2,0,1:T(8,128)} %copy.82) | data formatting | bytes 14548992 | tf_op jit(solution)/shard_map/reshape | solution.py:89
  83.3 2.0 slice.62
  85.4 9.0 %fusion.16 = (bf16[2,256,4096]{1,2,0:T(8,128)(2,1)S(1)}, f32[2,4096,256]{2,1,0:T(8,128)}) fusion(f32[2,4096,256]{2,1,0:T(8,128)} %fusion.27, bf16[2,222,4096]{2,1,0:T(8,128)(2,1)} %reshape.81, bf16[256,222]{0,1:T(8,128)(2,1)S(1)} %copy-done.10), kind=kOutput, calls=%fused_computation.37 | convolution fusion | flops 943718400 | bytes 24722432 | tf_op jit(solution)/shard_map/hc,mcn->mhn/dot_general | solution.py:75
  94.4 4.7 fusion.10
  99.1 2.0 copy-done.3
  101.1 2.0 fusion.21
  105.4 3.2 convert_element_type.74
  108.5 36.0 %all-gather.2.cloned.1.call-done = bf16[4,78,32,128]{3,2,1,0:T(8,128)(2,1)} async-done(((bf16[2,78,32,128]{3,2,1,0:T(8,128)(2,1)}), bf16[4,78,32,128]{3,2,1,0:T(8,128)(2,1)}) %all-gather.2.cloned.1.call-update) | async-done | bytes 2555920 | tf_op jit(solution)/shard_map/all_gather | solution.py:100
  144.6 4.8 convert_element_type.75
  149.4 24.0 %while.14 = (s32[]{:T(128)}, f32[2,78,32,128]{3,2,1,0:T(8,128)}, f32[4,78,32,128]{3,2,1,0:T(8,128)}, f32[2,78,32,128]{3,2,1,0:T(8,128)}, s32[]{:T(128)}, /*index=5*/s32[]{:T(128)}) while((s32[]{:T(128)}, f32[2,78,32,128]{3,2,1,0:T(8,128)}, f32[4,78,32,128]{3,2,1,0:T(8,128)}, f32[2,78,32,128]{3,2,1,0:T(8,128)}, s32[]{:T(128)}, ...), condition=%wide.region_1.2_spmd.clone, body=%wide.region_0.1_spmd.clone.sunk | while | flops 3833859 | bytes 11501651 | solution.py:106
  150.9 4.0 select_add_fusion.2
  156.3 4.8 select_add_fusion.2
  162.5 4.8 select_add_fusion.2
  168.7 4.8 select_add_fusion.2
  173.4 2.8 subtract_convert_fusion
  177.0 3.8 convolution_bitcast_fusion.4
  180.8 6.4 %fusion.6 = bf16[2,256,4096]{1,2,0:T(8,128)(2,1)S(1)} fusion(f32[2,4096,256]{2,1,0:T(8,128)} %get-tuple-element.147, bf16[2,78,4096]{2,1,0:T(8,128)(2,1)S(1)} %reshape.86, bf16[78,256,1]{1,0,2:T(8,128)(2,1)S(1)} %reshape.110), kind=kOutput, calls=%fused_computation.21 | convolution fusion | flops 346030080 | bytes 13900800 | tf_op jit(solution)/shard_map/ch,mcn->mhn/dot_general | solution.py:117
  187.2 2.0 convolution_bitcast_fusion.2
  189.3 3.5 fusion.5
  192.8 1.9 copy-done.4
  196.6 6.8 %convolution_bitcast_fusion = f32[2,222,4096]{2,1,0:T(8,128)} fusion(bf16[2,256,4096]{1,2,0:T(8,128)(2,1)} %copy-done.4, bf16[256,222]{0,1:T(8,128)(2,1)S(1)} %copy-done.10), kind=kOutput, calls=%fused_computation.42 | convolution fusion | flops 931135488 | bytes 11582464 | tf_op jit(solution)/shard_map/hc,mhn->mcn/dot_general | solution.py:134
  205.8 11.8 %copy.87 = f32[2,222,4096]{2,0,1:T(2,128)} copy(f32[2,222,4096]{2,1,0:T(8,128)} %convolution_bitcast_fusion) | data formatting | bytes 14548992 | tf_op jit(solution)/shard_map/hc,mhn->mcn/transpose | solution.py:134
  217.6 2.4 reshape.92
  220.0 1.9 copy.89
  221.9 16.4 %scatter_fusion = f32[2,6,37,4096]{3,0,2,1:T(2,128)} fusion(f32[2,6,37,4096]{3,0,2,1:T(2,128)} %bitcast.129, s32[13]{0:T(128)S(1)} %multiply_bitcast_fusion, f32[13,2,6,4096]{3,1,2,0:T(2,128)S(1)} %copy.89), kind=kCustom, calls=%fused_computation | custom fusion | flops 638976 | bytes 7667764 | tf_op jit(solution)/shard_map/scatter-add | solution.py:140
  238.4 10.9 %reshape.88 = f32[2,222,32,128]{3,2,0,1:T(8,128)} reshape(f32[2,6,37,4096]{3,0,2,1:T(2,128)} %scatter_fusion) | data formatting | bytes 14548992 | tf_op jit(solution)/shard_map/reshape | solution.py:144
  249.2 10.1 %copy.96 = f32[2,222,32,128]{1,2,3,0:T(8,128)} copy(f32[2,222,32,128]{3,2,0,1:T(8,128)} %reshape.88) | data formatting | bytes 14548992 | tf_op jit(solution)/shard_map/reshape | solution.py:144
  259.3 10.2 %multiply_reduce_fusion = (f32[222]{0:T(256)S(1)}, bf16[2,222,32,128]{1,2,3,0:T(8,128)(2,1)S(1)}) fusion(f32[2,222,32,128]{1,2,3,0:T(8,128)} %copy.96, f32[2,222,32,128]{1,2,3,0:T(8,128)} %get-tuple-element.133), kind=kLoop, calls=%fused_computation.40 | loop fusion | flops 5455650 | bytes 18187128 | tf_op jit(solution)/shard_map/reduce_sum | solution.py:147
  269.5 2.0 copy-done.1
  274.1 60.7 %all-reduce = (f32[256,16]{0,1:T(8,128)S(1)}, f32[222]{0:T(256)S(1)}) all-reduce(f32[256,16]{0,1:T(8,128)S(1)} %convolution_bitcast_fusion.5, f32[222]{0:T(256)S(1)} %get-tuple-element.134), channel_id=1, replica_groups=mesh['ens'=2,'lat'=4,'lon'=4] {'lat','lon'}, use_global_device_ids=true, to_apply=%region_5.6 | all-reduce | flops 4318 | bytes 34544 | tf_op jit(solution)/shard_map/psum | solution.py:149
  334.8 7.3 %all-reduce.2 = (f32[256,16]{0,1:T(8,128)S(1)}, f32[222]{0:T(256)S(1)}) all-reduce(f32[256,16]{0,1:T(8,128)S(1)} %get-tuple-element.121, f32[222]{0:T(256)S(1)} %get-tuple-element.122), channel_id=1, replica_groups=mesh['ens'=2,'lat'=4,'lon'=4] {'ens'}, use_global_device_ids=true, to_apply=%region_6.7 | all-reduce | flops 4318 | bytes 34544 | tf_op jit(solution)/shard_map/psum | solution.py:148
  344.0 3.8 collective-permute-start.7
  349.8 8.6 %convert_multiply_fusion = f32[2,222,34,130]{1,2,3,0:T(8,128)} fusion(bf16[2,222,34,1]{1,2,3,0:T(8,128)(2,1)S(1)} %collective-permute-done.7, bf16[2,222,1,128]{1,2,3,0:T(2,128)(2,1)S(1)} %copy.94, bf16[2,222,32,128]{1,2,3,0:T(8,128)(2,1)} %copy-done.1, bf16[2,222,1,128]{1,2,3,0:T(2,128)(2,1)S(1)} %copy.93, ...), kind=kLoop, calls=%fused_computation.4 | loop fusion | flops 21587280 | bytes 11775016 | tf_op jit(solution)/shard_map/mul | solution.py:42
  358.4 80.8 %all-reduce.7.cloned.1.call-done = (f32[256,222]{0,1:T(8,128)}, f32[256,256]{1,0:T(8,128)}, f32[78,256]{1,0:T(8,128)}) async-done(((f32[256,222]{0,1:T(8,128)}, f32[256,256]{1,0:T(8,128)}, f32[78,256]{1,0:T(8,128)}), (f32[256,222]{0,1:T(8,128)}, f32[256,256]{1,0:T(8,128)}, f32[78,256]{1,0:T(8,128)})) %all-reduce.7.cloned.1.call-update) | async-done | bytes 569360 | tf_op jit(solution)/shard_map/psum | solution.py:149
  440.8 19.4 %fusion.4 = bf16[2,222,32,128]{1,2,3,0:T(8,128)(2,1)} fusion(f32[2,222,32,128]{1,2,3,0:T(8,128)} %copy.96, f32[2,222,34,130]{1,2,3,0:T(8,128)} %convert_multiply_fusion, f32[222]{0:T(256)S(1)} %copy-done.12), kind=kLoop, calls=%fused_computation.12 | loop fusion | flops 14548992 | bytes 40010616 | tf_op jit(solution)/shard_map/convert_element_type | solution.py:157
  460.2 8.3 %copy.105 = bf16[2,222,32,128]{3,2,1,0:T(8,128)(2,1)} copy(bf16[2,222,32,128]{1,2,3,0:T(8,128)(2,1)} %fusion.4) | data formatting | bytes 7274496
  468.6 3.1 all-reduce.9.cloned.1.call-done
  (84 shorter events, 31.7 us)
Async XLA Ops:
  7.2 87.3 %copy-start = (bf16[256,256]{1,0:T(8,128)(2,1)S(1)}, bf16[256,256]{1,0:T(8,128)(2,1)}, u32[]{:S(2)}) copy-start(bf16[256,256]{1,0:T(8,128)(2,1)} %param.15) | copy-start | bytes 393220
  7.2 137.4 %all-gather.2.cloned.1.call-start = ((), (), s32[]{:S(2)}) async-start(), calls=%async_computation | async-start | bytes 3833856 | tf_op jit(solution)/shard_map/all_gather | solution.py:100
  9.1 17.2 %collective-permute-start = (bf16[2,222,1,128]{3,1,2,0:T(8,128)(2,1)S(1)}, bf16[2,222,1,128]{3,1,2,0:T(8,128)(2,1)S(1)}, u32[]{:S(2)}, u32[]{:S(2)}) collective-permute-start(bf16[2,222,1,128]{3,1,2,0:T(8,128)(2,1)S(1)} %copy.113), channel_id=1, source_target_pairs={{0,4},{4,8},{8,12},{12,0},{1,5},{5,9},{9,13},{13,1},{2,6},{6,10},{... | collective-permute-start | bytes 341000 | tf_op jit(solution)/shard_map/ppermute | solution.py:18
  9.7 16.8 %collective-permute-start.1 = (bf16[2,222,1,128]{3,1,2,0:T(8,128)(2,1)S(1)}, bf16[2,222,1,128]{3,1,2,0:T(8,128)(2,1)S(1)}, u32[]{:S(2)}, u32[]{:S(2)}) collective-permute-start(bf16[2,222,1,128]{3,1,2,0:T(8,128)(2,1)S(1)} %copy.114), channel_id=1, source_target_pairs={{4,0},{8,4},{12,8},{0,12},{5,1},{9,5},{13,9},{1,13},{6,2},{10,6},{... | collective-permute-start | bytes 341000 | tf_op jit(solution)/shard_map/ppermute | solution.py:21
  18.0 14.3 %copy-start.11 = (bf16[222,256]{1,0:T(8,128)(2,1)S(1)}, bf16[222,256]{1,0:T(8,128)(2,1)}, u32[]{:S(2)}) copy-start(bf16[222,256]{1,0:T(8,128)(2,1)} %param.16) | copy-start | bytes 340996
  27.5 6.5 %collective-permute-start.2 = (bf16[2,222,34,1]{1,2,3,0:T(8,128)(2,1)S(1)}, bf16[2,222,34,1]{1,2,3,0:T(8,128)(2,1)S(1)}, u32[]{:S(2)}, u32[]{:S(2)}) collective-permute-start(bf16[2,222,34,1]{1,2,3,0:T(8,128)(2,1)S(1)} %get-tuple-element.138), channel_id=1, source_target_pairs={{0,1},{1,2},{2,3},{3,0},{4,5},{5,6},{6,7},{7,4},{8,9},{9,10},{10,1... | collective-permute-start | bytes 90584 | tf_op jit(solution)/shard_map/ppermute | solution.py:18
  29.9 4.5 collective-permute-start.3
  32.4 6.8 %copy-start.12 = (f32[222]{0:T(256)S(1)}, f32[222]{0:T(256)}, u32[]{:S(2)}) copy-start(f32[222]{0:T(256)} %param.17) | copy-start | bytes 2668
  73.4 12.0 %copy-start.10 = (bf16[256,222]{0,1:T(8,128)(2,1)S(1)}, bf16[256,222]{0,1:T(8,128)(2,1)}, u32[]{:S(2)}) copy-start(bf16[256,222]{0,1:T(8,128)(2,1)} %param.13) | copy-start | bytes 340996
  94.4 4.7 copy-start.6
  99.1 2.0 copy-start.3
  104.8 334.5 %all-reduce.7.cloned.1.call-start = ((), (), s32[]{:S(2)}) async-start(), calls=%async_computation.1 | async-start | bytes 1146880 | tf_op jit(solution)/shard_map/psum | solution.py:149
  149.4 24.0 %copy-start.2 = (bf16[2,78,32,128]{3,2,1,0:T(8,128)(2,1)S(1)}, bf16[2,78,32,128]{3,2,1,0:T(8,128)(2,1)}, u32[]{:S(2)}) copy-start(bf16[2,78,32,128]{3,2,1,0:T(8,128)(2,1)} %reshape.85) | copy-start | bytes 3833860
  177.0 12.3 %slice-start = ((s8[8388608]{0:T(1024)(128)(4,1)}), s8[4194304]{0:T(1024)(128)(4,1)S(1)}, s32[]{:S(2)}) async-start(s8[8388608]{0:T(1024)(128)(4,1)} %bitcast.134), calls=%async_computation.3 | async-start | bytes 8388608
  180.8 6.4 %copy-start.7 = (bf16[2,256,4096]{1,2,0:T(8,128)(2,1)S(1)}, bf16[2,256,4096]{1,2,0:T(8,128)(2,1)}, u32[]{:S(2)}) copy-start(bf16[2,256,4096]{1,2,0:T(8,128)(2,1)} %copy-done.6) | copy-start | bytes 12582916
  180.8 8.4 %slice-start.1 = ((s8[8388608]{0:T(1024)(128)(4,1)}), s8[4194304]{0:T(1024)(128)(4,1)S(1)}, s32[]{:S(2)}) async-start(s8[8388608]{0:T(1024)(128)(4,1)} %bitcast.134), calls=%async_computation.4 | async-start | bytes 8388608
  189.2 5.5 %copy-start.9 = (bf16[2,222,4096]{2,1,0:T(8,128)(2,1)S(1)}, bf16[2,222,4096]{2,1,0:T(8,128)(2,1)}, u32[]{:S(2)}) copy-start(bf16[2,222,4096]{2,1,0:T(8,128)(2,1)} %reshape.81) | copy-start | bytes 10911748
  192.8 1.9 copy-start.4
  196.6 8.6 %copy-start.5 = (bf16[2,256,4096]{1,2,0:T(8,128)(2,1)S(1)}, bf16[2,256,4096]{1,2,0:T(8,128)(2,1)}, u32[]{:S(2)}) copy-start(bf16[2,256,4096]{1,2,0:T(8,128)(2,1)} %copy-done.4) | copy-start | bytes 12582916
  205.8 11.8 %copy-start.8 = (f32[2,78,32,128]{3,2,0,1:T(8,128)S(1)}, f32[2,78,32,128]{3,2,0,1:T(8,128)}, u32[]{:S(2)}) copy-start(f32[2,78,32,128]{3,2,0,1:T(8,128)} %copy.88) | copy-start | bytes 7667716
  269.5 2.0 copy-start.1
  272.1 70.6 %collective-permute-start.4 = (bf16[2,222,1,128]{3,1,2,0:T(8,128)(2,1)S(1)}, bf16[2,222,1,128]{3,1,2,0:T(8,128)(2,1)S(1)}, u32[]{:S(2)}, u32[]{:S(2)}) collective-permute-start(bf16[2,222,1,128]{3,1,2,0:T(8,128)(2,1)S(1)} %copy.91), channel_id=1, source_target_pairs={{0,4},{4,8},{8,12},{12,0},{1,5},{5,9},{9,13},{13,1},{2,6},{6,10},{... | collective-permute-start | bytes 341000 | tf_op jit(solution)/shard_map/ppermute | solution.py:18
  272.4 70.6 %collective-permute-start.5 = (bf16[2,222,1,128]{3,1,2,0:T(8,128)(2,1)S(1)}, bf16[2,222,1,128]{3,1,2,0:T(8,128)(2,1)S(1)}, u32[]{:S(2)}, u32[]{:S(2)}) collective-permute-start(bf16[2,222,1,128]{3,1,2,0:T(8,128)(2,1)S(1)} %copy.92), channel_id=1, source_target_pairs={{4,0},{8,4},{12,8},{0,12},{5,1},{9,5},{13,9},{1,13},{6,2},{10,6},{... | collective-permute-start | bytes 341000 | tf_op jit(solution)/shard_map/ppermute | solution.py:21
  344.0 5.9 %collective-permute-start.6 = (bf16[2,222,34,1]{1,2,3,0:T(8,128)(2,1)S(1)}, bf16[2,222,34,1]{1,2,3,0:T(8,128)(2,1)S(1)}, u32[]{:S(2)}, u32[]{:S(2)}) collective-permute-start(bf16[2,222,34,1]{1,2,3,0:T(8,128)(2,1)S(1)} %get-tuple-element.136), channel_id=1, source_target_pairs={{0,1},{1,2},{2,3},{3,0},{4,5},{5,6},{6,7},{7,4},{8,9},{9,10},{10,1... | collective-permute-start | bytes 90584 | tf_op jit(solution)/shard_map/ppermute | solution.py:18
  344.0 5.8 %collective-permute-start.7 = (bf16[2,222,34,1]{1,2,3,0:T(8,128)(2,1)S(1)}, bf16[2,222,34,1]{1,2,3,0:T(8,128)(2,1)S(1)}, u32[]{:S(2)}, u32[]{:S(2)}) collective-permute-start(bf16[2,222,34,1]{1,2,3,0:T(8,128)(2,1)S(1)} %get-tuple-element.137), channel_id=1, source_target_pairs={{1,0},{2,1},{3,2},{0,3},{5,4},{6,5},{7,6},{4,7},{9,8},{10,9},{11,1... | collective-permute-start | bytes 90584 | tf_op jit(solution)/shard_map/ppermute | solution.py:21
  348.4 123.3 %all-reduce.9.cloned.1.call-start = ((), (), s32[]{:S(2)}) async-start(), calls=%async_computation.2 | async-start | bytes 1196032 | tf_op jit(solution)/shard_map/psum | solution.py:148
Sparse Core Ops, SparseCore 0:
  104.9 39.6 all-gather.1
  348.6 90.6 all-reduce.6
  442.3 29.3 all-reduce.8
